TPU v7x, 32 devices: a whole 2x2x4 slice. The times are simulated.
32 devices in a mesh: context: 8 (over y, x, core), tensor: 4 (over z).
Axes of the slice: x: 2, y: 2, z: 4, core: 2. Of those that a mesh axis runs over, the one named last changes fastest.
Arguments:
- block_input: bfloat16 [4, 4096, 2048], P(None, 'context'), may hold values from -6 to 6
- doc_lengths: int32 [4, 8], replicated, may hold values from 0 to 4096, as said below
- norm_gains: bfloat16 [2, 2048], P(None, 'context'), may hold values from 0.099609375 to 1.8984375
- qkv_weight: bfloat16 [3, 2048, 2048], P(None, 'context', 'tensor'), may hold values from -0.125 to 0.125
- out_weight: bfloat16 [2048, 2048], P('tensor', 'context'), may hold values from -1 to 1
- gateup_weight: bfloat16 [2, 2048, 4096], P(None, 'context', 'tensor'), may hold values from -0.125 to 0.125
- down_weight: bfloat16 [4096, 2048], P('tensor', 'context'), may hold values from -0.09375 to 0.09375
- cotangent: bfloat16 [4, 4096, 2048], P(None, 'context'), may hold values from -6 to 6
Outputs:
- block_output: bfloat16 [4, 4096, 2048], P(None, 'context')
- input_grad: float32 [4, 4096, 2048], P(None, 'context')
- gains_grad: float32 [2, 2048], P(None, 'context')
- qkv_grad: float32 [3, 2048, 2048], P(None, 'context', 'tensor')
- out_grad: float32 [2048, 2048], P('tensor', 'context')
- gateup_grad: float32 [2, 2048, 4096], P(None, 'context', 'tensor')
- down_grad: float32 [4096, 2048], P('tensor', 'context')
Inputs may be any that keep to these rules, and one draw needn't show every extreme that they name: `doc_lengths`: each row sums to 4096. In each micro-batch, rows m * 2 to m * 2 + 1, one row drawn from the seed is a single document of 4096 tokens followed by zeros; every other row holds 8 documents of one token or more.
All inputs are finite; a program needn't handle non-finite values.
Results may differ from a plain program's by a relative error of at most 0.024.
Values may be sent and summed in bfloat16 or wider, within the bound.
No kernel may reach another device: no remote copies, remote signals or barrier semaphores. Data moves between devices by JAX's collectives and lax.ppermute only.
A program may use at most 576 MiB of HBM per device.

v0:
```python
import math
import jax
import jax.numpy as jnp
from jax import lax
from jax.sharding import PartitionSpec as P

HEAD_DIM = 64
WINDOW = 2048
SEQ_LEN = 4096
SB = 2
epsilon = 1e-05
rope_base = 10000.0
masked_fill = -1e30


def rope_tables(positions, head_dim):
    half_dim = head_dim // 2
    counter = jnp.arange(half_dim, dtype=jnp.float32)
    frequency = jnp.exp(counter * (-2.0 * math.log(rope_base) / head_dim))
    angles = positions.astype(jnp.float32)[:, None] * frequency[None, :]
    return (jnp.cos(angles)[:, None, :], jnp.sin(angles)[:, None, :])


def rotate(values, cosine, sine):
    half_dim = values.shape[-1] // 2
    front_half = values[..., :half_dim]
    back_half = values[..., half_dim:]
    return jnp.concatenate(
        [front_half * cosine - back_half * sine, back_half * cosine + front_half * sine], axis=-1
    )


def unrotate(values, cosine, sine):
    half_dim = values.shape[-1] // 2
    front_half = values[..., :half_dim]
    back_half = values[..., half_dim:]
    return jnp.concatenate(
        [front_half * cosine + back_half * sine, back_half * cosine - front_half * sine], axis=-1
    )


def norm_forward(rows, gain):
    inverse = lax.rsqrt(jnp.mean(rows * rows, axis=-1, keepdims=True) + epsilon)
    normal = rows * inverse
    return (normal, inverse, normal * gain)


def norm_backward(grad_normed, normal, inverse, gain):
    grad_normal = grad_normed * gain
    inner = jnp.mean(grad_normal * normal, axis=-1, keepdims=True)
    return (inverse * (grad_normal - normal * inner), jnp.sum(grad_normed * normal, axis=(0, 1)))


def shards(
    block_input,
    doc_lengths,
    norm_gains,
    qkv_weight,
    out_weight,
    gateup_weight,
    down_weight,
    cotangent,
):
    local_len = block_input.shape[1]
    model_width = block_input.shape[2]
    device_index = lax.axis_index("context")
    key_span = WINDOW + local_len
    head_width = qkv_weight.shape[2]
    local_heads = head_width // HEAD_DIM
    hidden_width = gateup_weight.shape[2]
    micro_count = block_input.shape[0] // SB
    score_scale = HEAD_DIM ** (-0.5)
    local_start = device_index * local_len
    query_pos = local_start + jnp.arange(local_len, dtype=jnp.int32)
    key_pos = local_start - WINDOW + jnp.arange(key_span, dtype=jnp.int32)
    cosine, sine = rope_tables(query_pos, HEAD_DIM)
    seq_positions = jnp.arange(SEQ_LEN, dtype=jnp.int32)
    distance = query_pos[:, None] - key_pos[None, :]
    in_window = (distance >= 0) & (distance < WINDOW)

    def micro_step(micro_index, carried):
        output_all, input_grads, total_qkv, total_out, total_gateup, total_down, total_gains = (
            carried
        )
        qkv_full, out_full, gateup_full, down_full, gains_full = (
            lax.all_gather(qkv_weight, "context", axis=1, tiled=True),
            lax.all_gather(out_weight, "context", axis=1, tiled=True),
            lax.all_gather(gateup_weight, "context", axis=1, tiled=True),
            lax.all_gather(down_weight, "context", axis=1, tiled=True),
            lax.all_gather(norm_gains, "context", axis=1, tiled=True),
        )
        gains_value = gains_full.astype(jnp.float32)
        first_row = micro_index * SB
        rows_in = lax.dynamic_slice_in_dim(block_input, first_row, SB, 0).astype(jnp.float32)
        incoming = lax.dynamic_slice_in_dim(cotangent, first_row, SB, 0)
        lengths = lax.dynamic_slice_in_dim(doc_lengths, first_row, SB, 0)
        doc_ends = jnp.cumsum(lengths, axis=1)
        segment = jnp.sum(
            (seq_positions[None, :, None] >= doc_ends[:, None, :]).astype(jnp.int32), axis=-1
        )
        padded_seg = jnp.concatenate([jnp.full((SB, WINDOW), -1, jnp.int32), segment], axis=1)
        key_seg = lax.dynamic_slice_in_dim(padded_seg, local_start, key_span, 1)
        query_seg = lax.dynamic_slice_in_dim(segment, local_start, local_len, 1)
        visible = ((query_seg[:, :, None] == key_seg[:, None, :]) & in_window[None])[:, None]
        normal_one, inverse_one, normed_one = norm_forward(rows_in, gains_value[0])
        normed_one = normed_one.astype(jnp.bfloat16)
        projected = jnp.einsum(
            "snd,kde->ksne", normed_one, qkv_full, preferred_element_type=jnp.float32
        )
        projected = projected.reshape(3, SB, local_len, local_heads, HEAD_DIM)
        queries = rotate(projected[0], cosine, sine).astype(jnp.bfloat16)
        key_rows = rotate(projected[1], cosine, sine).astype(jnp.bfloat16)
        value_rows = projected[2].astype(jnp.bfloat16)
        key_value = jnp.stack([key_rows, value_rows]).reshape(2, SB, local_len, head_width)
        all_pairs = lax.all_gather(key_value, "context", axis=2, tiled=True)
        padded_pairs = jnp.concatenate(
            [jnp.zeros((2, SB, WINDOW, head_width), jnp.bfloat16), all_pairs], axis=2
        )
        window_pairs = lax.dynamic_slice_in_dim(padded_pairs, local_start, key_span, 2)
        window_pairs = window_pairs.reshape(2, SB, key_span, local_heads, HEAD_DIM)
        key_buffer = window_pairs[0]
        value_buffer = window_pairs[1]
        scores = (
            jnp.einsum("sqhe,skhe->shqk", queries, key_buffer, preferred_element_type=jnp.float32)
            * score_scale
        )
        scores = jnp.where(visible, scores, masked_fill)
        row_max = jnp.max(scores, axis=-1, keepdims=True)
        exp_scores = jnp.exp(scores - row_max)
        row_total = jnp.sum(exp_scores, axis=-1, keepdims=True)
        log_total = row_max + jnp.log(row_total)
        probs_low = (exp_scores / row_total).astype(jnp.bfloat16)
        attended = jnp.einsum(
            "shqk,skhe->sqhe", probs_low, value_buffer, preferred_element_type=jnp.float32
        )
        attended = attended.reshape(SB, local_len, head_width).astype(jnp.bfloat16)
        attention_part = jnp.einsum(
            "snc,cd->snd", attended, out_full, preferred_element_type=jnp.float32
        )
        attention_branch = lax.psum(attention_part.astype(jnp.bfloat16), "tensor").astype(
            jnp.float32
        )
        hidden = rows_in + attention_branch
        normal_two, inverse_two, normed_two = norm_forward(hidden, gains_value[1])
        normed_two = normed_two.astype(jnp.bfloat16)
        gate_up = jnp.einsum(
            "snd,kdf->ksnf", normed_two, gateup_full, preferred_element_type=jnp.float32
        )
        gate_sigmoid = jax.nn.sigmoid(gate_up[0])
        gate_silu = gate_up[0] * gate_sigmoid
        activation = (gate_silu * gate_up[1]).astype(jnp.bfloat16)
        feedforward_part = jnp.einsum(
            "snf,fd->snd", activation, down_full, preferred_element_type=jnp.float32
        )
        feedforward_branch = lax.psum(feedforward_part.astype(jnp.bfloat16), "tensor").astype(
            jnp.float32
        )
        result = (hidden + feedforward_branch).astype(jnp.bfloat16)
        total_down = total_down + jnp.einsum(
            "snf,snd->fd", activation, incoming, preferred_element_type=jnp.float32
        )
        grad_activation = jnp.einsum(
            "snd,fd->snf", incoming, down_full, preferred_element_type=jnp.float32
        )
        grad_gate = (
            grad_activation * gate_up[1] * gate_sigmoid * (1.0 + gate_up[0] * (1.0 - gate_sigmoid))
        )
        grad_up = grad_activation * gate_silu
        grad_gateup = jnp.stack([grad_gate, grad_up]).astype(jnp.bfloat16)
        total_gateup = total_gateup + jnp.einsum(
            "snd,ksnf->kdf", normed_two, grad_gateup, preferred_element_type=jnp.float32
        )
        second_part = jnp.einsum(
            "ksnf,kdf->snd", grad_gateup, gateup_full, preferred_element_type=jnp.float32
        )
        grad_normed_two = lax.psum(second_part.astype(jnp.bfloat16), "tensor").astype(jnp.float32)
        grad_rows_two, gain_two = norm_backward(
            grad_normed_two, normal_two, inverse_two, gains_value[1]
        )
        grad_hidden = incoming.astype(jnp.float32) + grad_rows_two
        grad_hidden_low = grad_hidden.astype(jnp.bfloat16)
        total_out = total_out + jnp.einsum(
            "snc,snd->cd", attended, grad_hidden_low, preferred_element_type=jnp.float32
        )
        grad_attended = jnp.einsum(
            "snd,cd->snc", grad_hidden_low, out_full, preferred_element_type=jnp.float32
        )
        grad_attended = grad_attended.astype(jnp.bfloat16).reshape(
            SB, local_len, local_heads, HEAD_DIM
        )
        again = (
            jnp.einsum("sqhe,skhe->shqk", queries, key_buffer, preferred_element_type=jnp.float32)
            * score_scale
        )
        again = jnp.where(visible, again, masked_fill)
        probs = jnp.exp(again - log_total)
        probs_again = probs.astype(jnp.bfloat16)
        grad_probs = jnp.einsum(
            "sqhe,skhe->shqk", grad_attended, value_buffer, preferred_element_type=jnp.float32
        )
        row_dot = jnp.sum(probs * grad_probs, axis=-1, keepdims=True)
        grad_scores = (probs * (grad_probs - row_dot)).astype(jnp.bfloat16)
        grad_queries = (
            jnp.einsum(
                "shqk,skhe->sqhe", grad_scores, key_buffer, preferred_element_type=jnp.float32
            )
            * score_scale
        )
        grad_keys = (
            jnp.einsum("shqk,sqhe->skhe", grad_scores, queries, preferred_element_type=jnp.float32)
            * score_scale
        )
        grad_values = jnp.einsum(
            "shqk,sqhe->skhe", probs_again, grad_attended, preferred_element_type=jnp.float32
        )
        grad_pairs = jnp.stack([grad_keys, grad_values]).reshape(2, SB, key_span, head_width)
        spread = jnp.zeros((2, SB, WINDOW + SEQ_LEN, head_width), jnp.float32)
        spread = lax.dynamic_update_slice_in_dim(spread, grad_pairs, local_start, 2)[:, :, WINDOW:]
        grad_own = lax.psum_scatter(
            spread.astype(jnp.bfloat16), "context", scatter_dimension=2, tiled=True
        ).astype(jnp.float32)
        grad_own = grad_own.reshape(2, SB, local_len, local_heads, HEAD_DIM)
        grad_projected = jnp.stack(
            [unrotate(grad_queries, cosine, sine), unrotate(grad_own[0], cosine, sine), grad_own[1]]
        )
        grad_projected = grad_projected.reshape(3, SB, local_len, head_width).astype(jnp.bfloat16)
        total_qkv = total_qkv + jnp.einsum(
            "snd,ksne->kde", normed_one, grad_projected, preferred_element_type=jnp.float32
        )
        first_part = jnp.einsum(
            "ksne,kde->snd", grad_projected, qkv_full, preferred_element_type=jnp.float32
        )
        grad_normed_one = lax.psum(first_part.astype(jnp.bfloat16), "tensor").astype(jnp.float32)
        grad_rows_one, gain_one = norm_backward(
            grad_normed_one, normal_one, inverse_one, gains_value[0]
        )
        grad_input = grad_hidden + grad_rows_one
        total_gains = total_gains + jnp.stack([gain_one, gain_two])
        output_all = lax.dynamic_update_slice_in_dim(output_all, result, first_row, 0)
        input_grads = lax.dynamic_update_slice_in_dim(input_grads, grad_input, first_row, 0)
        return (
            output_all,
            input_grads,
            total_qkv,
            total_out,
            total_gateup,
            total_down,
            total_gains,
        )

    initial = (
        jnp.zeros(block_input.shape, jnp.bfloat16),
        jnp.zeros(block_input.shape, jnp.float32),
        jnp.zeros((3, model_width, head_width), jnp.float32),
        jnp.zeros((head_width, model_width), jnp.float32),
        jnp.zeros((2, model_width, hidden_width), jnp.float32),
        jnp.zeros((hidden_width, model_width), jnp.float32),
        jnp.zeros((2, model_width), jnp.float32),
    )
    final = lax.fori_loop(0, micro_count, micro_step, initial)
    gains_grad, qkv_grad, out_grad, gateup_grad, down_grad = (
        lax.psum_scatter(
            final[6].astype(jnp.bfloat16), "context", scatter_dimension=1, tiled=True
        ).astype(jnp.float32),
        lax.psum_scatter(
            final[2].astype(jnp.bfloat16), "context", scatter_dimension=1, tiled=True
        ).astype(jnp.float32),
        lax.psum_scatter(
            final[3].astype(jnp.bfloat16), "context", scatter_dimension=1, tiled=True
        ).astype(jnp.float32),
        lax.psum_scatter(
            final[4].astype(jnp.bfloat16), "context", scatter_dimension=1, tiled=True
        ).astype(jnp.float32),
        lax.psum_scatter(
            final[5].astype(jnp.bfloat16), "context", scatter_dimension=1, tiled=True
        ).astype(jnp.float32),
    )
    return (final[0], final[1], gains_grad, qkv_grad, out_grad, gateup_grad, down_grad)


def solution(mesh):
    in_specs = (
        P(None, "context", None),
        P(),
        P(None, "context"),
        P(None, "context", "tensor"),
        P("tensor", "context"),
        P(None, "context", "tensor"),
        P("tensor", "context"),
        P(None, "context", None),
    )
    out_specs = (
        P(None, "context", None),
        P(None, "context", None),
        P(None, "context"),
        P(None, "context", "tensor"),
        P("tensor", "context"),
        P(None, "context", "tensor"),
        P("tensor", "context"),
    )
    return jax.shard_map(shards, mesh=mesh, in_specs=in_specs, out_specs=out_specs, check_vma=False)
```

profile of v0, /device:TPU:0, one launch (start us, length us, event | category | flops | bytes accessed | tf_op | source)
XLA Modules:
  0.0 3081.5 jit_solution(3677816356305977269)
XLA Ops:
  24.9 2768.9 %while.30 = (s32[]{:T(128)}, bf16[4,512,2048]{2,1,0:T(8,128)(2,1)}, f32[4,512,2048]{2,1,0:T(8,128)}, f32[3,2048,512]{1,2,0:T(8,128)}, f32[512,2048]{1,0:T(8,128)...) while((s32[]{:T(128)}, bf16[4,512,2048]{2,1,0:T(8,128)(2,1)}, ...), condition=%wide.region_17.18_spmd.clone.clone.clone, body=%wide.region_0.17_spmd.clone.clone.clone.sunk | while | flops 81181999104 | bytes 1911083520 | solution.py:260
  41.3 35.8 %all-gather.8.cloned.1.call-done = bf16[3,2048,512]{1,2,0:T(8,128)(2,1)} async-done(((bf16[3,256,512]{1,2,0:T(8,128)(2,1)}), bf16[3,2048,512]{1,2,0:T(8,128)(2,1)}) %all-gather.8.cloned.1.call-update) | async-done | bytes 6291472 | tf_op jit(solution)/shard_map/while/body/eval_jaxpr/all_gather | solution.py:86
  97.7 86.7 %all-gather.10.cloned.1.call-done = bf16[2,2,4096,512]{2,3,0,1:T(8,128)(2,1)} async-done(((bf16[2,2,512,512]{2,3,0,1:T(8,128)(2,1)}), bf16[2,2,4096,512]{2,3,0,1:T(8,128)(2,1)}) %all-gather.10.cloned.1.call-update) | async-done | bytes 16777232 | tf_op jit(solution)/shard_map/while/body/eval_jaxpr/all_gather | solution.py:115
  288.7 156.5 %all-reduce.9.cloned.1.call-done = bf16[2,512,2048]{2,1,0:T(8,128)(2,1)} async-done(((bf16[2,512,2048]{2,1,0:T(8,128)(2,1)}), bf16[2,512,2048]{2,1,0:T(8,128)(2,1)}) %all-reduce.9.cloned.1.call-update) | async-done | bytes 4194320 | tf_op jit(solution)/shard_map/while/body/eval_jaxpr/psum | solution.py:140
  450.1 50.3 %all-gather.6.cloned.1.call-done = bf16[2,2048,1024]{2,1,0:T(8,128)(2,1)} async-done(((bf16[2,256,1024]{2,1,0:T(8,128)(2,1)}), bf16[2,2048,1024]{2,1,0:T(8,128)(2,1)}) %all-gather.6.cloned.1.call-update) | async-done | bytes 8388624 | tf_op jit(solution)/shard_map/while/body/eval_jaxpr/all_gather | solution.py:88
  565.5 155.0 %all-reduce.11.cloned.1.call-done = bf16[2,512,2048]{2,1,0:T(8,128)(2,1)} async-done(((bf16[2,512,2048]{2,1,0:T(8,128)(2,1)}), bf16[2,512,2048]{2,1,0:T(8,128)(2,1)}) %all-reduce.11.cloned.1.call-update) | async-done | bytes 4194320 | tf_op jit(solution)/shard_map/while/body/eval_jaxpr/psum | solution.py:176
  738.4 53.9 %multiply_reduce_fusion.5 = (f32[2,8,512]{2,1,0:T(8,128)S(1)}, f32[2,8,512,2560]{3,2,1,0:T(8,128)}) fusion(f32[2,8,512,2560]{3,2,1,0:T(8,128)} %get-tuple-element.1011, f32[2,8,512]{2,1,0:T(8,128)S(1)} %log_add_fusion.2, bf16[2,512,8,64]{1,3,2,0:T(8,128)(2,1)S(1)} %bitcast.269, bf16[2,2560,8,64]{1,3,2,0:T(8,128)(2,1)S(1)} %bitcast.265), kind=kOutput, calls=%fused_computation.5.clone.1 | convolution fusion | flops 2747260928 | bytes 174129152 | tf_op jit(solution)/shard_map/while/body/eval_jaxpr/sqhe,skhe->shqk/dot_general | solution.py:198
  823.3 66.5 %multiply_convert_fusion.8 = bf16[2,8,512,2560]{3,2,1,0:T(8,128)(2,1)} fusion(f32[2,8,512,2560]{3,2,1,0:T(8,128)} %get-tuple-element.1018, f32[2,8,512,2560]{3,2,1,0:T(8,128)} %get-tuple-element.1011, f32[2,8,512]{2,1,0:T(8,128)S(1)} %get-tuple-element.1019, f32[2,8,512]{2,1,0:T(8,128)S(1)} %log_add_fusion.2), kind=kLoop, calls=%fused_computation.4.clone.1 | loop fusion | flops 83886080 | bytes 209780736 | tf_op jit(solution)/shard_map/while/body/eval_jaxpr/convert_element_type | solution.py:202
  988.3 82.6 %reduce-scatter.19.cloned.1.call-done = bf16[2,2,512,512]{3,2,0,1:T(8,128)(2,1)} async-done(((bf16[2,2,4096,512]{3,2,0,1:T(8,128)(2,1)}), bf16[2,2,512,512]{3,2,0,1:T(8,128)(2,1)}) %reduce-scatter.19.cloned.1.call-update) | async-done | bytes 2097168 | tf_op jit(solution)/shard_map/while/body/eval_jaxpr/reduce_scatter | solution.py:219
  1137.2 247.5 %all-reduce.13.cloned.1.call-done = (bf16[2,512,2048]{2,1,0:T(8,128)(2,1)}, bf16[2,512,2048]{2,1,0:T(8,128)(2,1)}) async-done(((bf16[2,512,2048]{2,1,0:T(8,128)(2,1)}, bf16[2,512,2048]{2,1,0:T(8,128)(2,1)}), (bf16[2,512,2048]{2,1,0:T(8,128)(2,1)}, bf16[2,512,2048]{2,1,0:T(8,128)(2,1)})) %all-reduce.13.cloned.1.call-update) | async-done | bytes 8388624 | tf_op jit(solution)/shard_map/while/body/eval_jaxpr/psum | solution.py:155
  1424.9 33.7 %all-gather.8.cloned.1.call-done = bf16[3,2048,512]{1,2,0:T(8,128)(2,1)} async-done(((bf16[3,256,512]{1,2,0:T(8,128)(2,1)}), bf16[3,2048,512]{1,2,0:T(8,128)(2,1)}) %all-gather.8.cloned.1.call-update) | async-done | bytes 6291472 | tf_op jit(solution)/shard_map/while/body/eval_jaxpr/all_gather | solution.py:86
  1478.7 87.1 %all-gather.10.cloned.1.call-done = bf16[2,2,4096,512]{2,3,0,1:T(8,128)(2,1)} async-done(((bf16[2,2,512,512]{2,3,0,1:T(8,128)(2,1)}), bf16[2,2,4096,512]{2,3,0,1:T(8,128)(2,1)}) %all-gather.10.cloned.1.call-update) | async-done | bytes 16777232 | tf_op jit(solution)/shard_map/while/body/eval_jaxpr/all_gather | solution.py:115
  1573.0 32.9 %fusion.193 = (f32[2,8,512]{2,1,0:T(8,128)S(1)}, f32[2,8,512,2560]{3,2,1,0:T(8,128)}) fusion(bf16[2,2560,8,64]{1,3,2,0:T(8,128)(2,1)} %bitcast.256, bf16[2,512,8,32]{1,3,2,0:T(8,128)(2,1)} %get-tuple-element.1009, bf16[2,512,8,32]{1,3,2,0:T(8,128)(2,1)S(1)} %get-tuple-element.1010, pred[2,512,2560]{2,1,0:T(8,128)(4,1)S(1)} %compare_and_fusion.2), kind=kOutput, calls=%fused_computation.143.clone.1 | convolution fusion | flops 2749358080 | bytes 92831744 | tf_op jit(solution)/shard_map/while/body/eval_jaxpr/sqhe,skhe->shqk/dot_general | solution.py:124
  1670.2 156.4 %all-reduce.9.cloned.1.call-done = bf16[2,512,2048]{2,1,0:T(8,128)(2,1)} async-done(((bf16[2,512,2048]{2,1,0:T(8,128)(2,1)}), bf16[2,512,2048]{2,1,0:T(8,128)(2,1)}) %all-reduce.9.cloned.1.call-update) | async-done | bytes 4194320 | tf_op jit(solution)/shard_map/while/body/eval_jaxpr/psum | solution.py:140
  1831.5 50.3 %all-gather.6.cloned.1.call-done = bf16[2,2048,1024]{2,1,0:T(8,128)(2,1)} async-done(((bf16[2,256,1024]{2,1,0:T(8,128)(2,1)}), bf16[2,2048,1024]{2,1,0:T(8,128)(2,1)}) %all-gather.6.cloned.1.call-update) | async-done | bytes 8388624 | tf_op jit(solution)/shard_map/while/body/eval_jaxpr/all_gather | solution.py:88
  1946.9 155.0 %all-reduce.11.cloned.1.call-done = bf16[2,512,2048]{2,1,0:T(8,128)(2,1)} async-done(((bf16[2,512,2048]{2,1,0:T(8,128)(2,1)}), bf16[2,512,2048]{2,1,0:T(8,128)(2,1)}) %all-reduce.11.cloned.1.call-update) | async-done | bytes 4194320 | tf_op jit(solution)/shard_map/while/body/eval_jaxpr/psum | solution.py:176
  2119.6 53.9 %multiply_reduce_fusion.5 = (f32[2,8,512]{2,1,0:T(8,128)S(1)}, f32[2,8,512,2560]{3,2,1,0:T(8,128)}) fusion(f32[2,8,512,2560]{3,2,1,0:T(8,128)} %get-tuple-element.1011, f32[2,8,512]{2,1,0:T(8,128)S(1)} %log_add_fusion.2, bf16[2,512,8,64]{1,3,2,0:T(8,128)(2,1)S(1)} %bitcast.269, bf16[2,2560,8,64]{1,3,2,0:T(8,128)(2,1)S(1)} %bitcast.265), kind=kOutput, calls=%fused_computation.5.clone.1 | convolution fusion | flops 2747260928 | bytes 174129152 | tf_op jit(solution)/shard_map/while/body/eval_jaxpr/sqhe,skhe->shqk/dot_general | solution.py:198
  2204.5 66.6 %multiply_convert_fusion.8 = bf16[2,8,512,2560]{3,2,1,0:T(8,128)(2,1)} fusion(f32[2,8,512,2560]{3,2,1,0:T(8,128)} %get-tuple-element.1018, f32[2,8,512,2560]{3,2,1,0:T(8,128)} %get-tuple-element.1011, f32[2,8,512]{2,1,0:T(8,128)S(1)} %get-tuple-element.1019, f32[2,8,512]{2,1,0:T(8,128)S(1)} %log_add_fusion.2), kind=kLoop, calls=%fused_computation.4.clone.1 | loop fusion | flops 83886080 | bytes 209780736 | tf_op jit(solution)/shard_map/while/body/eval_jaxpr/convert_element_type | solution.py:202
  2369.6 82.6 %reduce-scatter.19.cloned.1.call-done = bf16[2,2,512,512]{3,2,0,1:T(8,128)(2,1)} async-done(((bf16[2,2,4096,512]{3,2,0,1:T(8,128)(2,1)}), bf16[2,2,512,512]{3,2,0,1:T(8,128)(2,1)}) %reduce-scatter.19.cloned.1.call-update) | async-done | bytes 2097168 | tf_op jit(solution)/shard_map/while/body/eval_jaxpr/reduce_scatter | solution.py:219
  2526.4 239.7 %all-reduce.13.cloned.1.call-done = (bf16[2,512,2048]{2,1,0:T(8,128)(2,1)}, bf16[2,512,2048]{2,1,0:T(8,128)(2,1)}) async-done(((bf16[2,512,2048]{2,1,0:T(8,128)(2,1)}, bf16[2,512,2048]{2,1,0:T(8,128)(2,1)}), (bf16[2,512,2048]{2,1,0:T(8,128)(2,1)}, bf16[2,512,2048]{2,1,0:T(8,128)(2,1)})) %all-reduce.13.cloned.1.call-update) | async-done | bytes 8388624 | tf_op jit(solution)/shard_map/while/body/eval_jaxpr/psum | solution.py:155
  2832.7 43.7 %reduce-scatter.11.cloned.1.call-done = bf16[512,256]{1,0:T(8,128)(2,1)} async-done(((bf16[512,2048]{1,0:T(8,128)(2,1)}), bf16[512,256]{1,0:T(8,128)(2,1)}) %reduce-scatter.11.cloned.1.call-update) | async-done | bytes 262160 | tf_op jit(solution)/shard_map/reduce_scatter | solution.py:268
  2878.1 52.7 %reduce-scatter.15.cloned.1.call-done = bf16[1024,256]{1,0:T(8,128)(2,1)} async-done(((bf16[1024,2048]{1,0:T(8,128)(2,1)}), bf16[1024,256]{1,0:T(8,128)(2,1)}) %reduce-scatter.15.cloned.1.call-update) | async-done | bytes 524304 | tf_op jit(solution)/shard_map/reduce_scatter | solution.py:274
  2932.9 63.3 %reduce-scatter.9.cloned.1.call-done = bf16[3,256,512]{2,1,0:T(8,128)(2,1)} async-done(((bf16[3,2048,512]{2,1,0:T(8,128)(2,1)}), bf16[3,256,512]{2,1,0:T(8,128)(2,1)}) %reduce-scatter.9.cloned.1.call-update) | async-done | bytes 786448 | tf_op jit(solution)/shard_map/reduce_scatter | solution.py:265
  2998.6 72.2 %reduce-scatter.13.cloned.1.call-done = bf16[2,256,1024]{2,1,0:T(8,128)(2,1)} async-done(((bf16[2,2048,1024]{2,1,0:T(8,128)(2,1)}), bf16[2,256,1024]{2,1,0:T(8,128)(2,1)}) %reduce-scatter.13.cloned.1.call-update) | async-done | bytes 1048592 | tf_op jit(solution)/shard_map/reduce_scatter | solution.py:271
  (373 shorter events, 936.6 us)
Async XLA Ops:
  24.9 52.3 %all-gather.8.cloned.1.call-start = ((), (), s32[]{:S(2)}) async-start(), calls=%async_computation.12 | async-start | bytes 7077888 | tf_op jit(solution)/shard_map/while/body/eval_jaxpr/all_gather | solution.py:86
  25.6 158.7 %all-gather.10.cloned.1.call-start = ((), (), s32[]{:S(2)}) async-start(), calls=%async_computation.13 | async-start | bytes 18874368 | tf_op jit(solution)/shard_map/while/body/eval_jaxpr/all_gather | solution.py:115
  91.1 190.1 %all-gather.12.cloned.1.call-start = ((), (), s32[]{:S(2)}) async-start(), calls=%async_computation.14 | async-start | bytes 2359296 | tf_op jit(solution)/shard_map/while/body/eval_jaxpr/all_gather | solution.py:87
  91.8 353.3 %all-reduce.9.cloned.1.call-start = ((), (), s32[]{:S(2)}) async-start(), calls=%async_computation.15 | async-start | bytes 8388608 | tf_op jit(solution)/shard_map/while/body/eval_jaxpr/psum | solution.py:140
  287.5 212.9 %all-gather.6.cloned.1.call-start = ((), (), s32[]{:S(2)}) async-start(), calls=%async_computation.11 | async-start | bytes 9437184 | tf_op jit(solution)/shard_map/while/body/eval_jaxpr/all_gather | solution.py:88
  288.1 251.5 %all-gather.14.cloned.1.call-start = ((), (), s32[]{:S(2)}) async-start(), calls=%async_computation.16 | async-start | bytes 4718592 | tf_op jit(solution)/shard_map/while/body/eval_jaxpr/all_gather | solution.py:89
  288.7 431.8 %all-reduce.11.cloned.1.call-start = ((), (), s32[]{:S(2)}) async-start(), calls=%async_computation.17 | async-start | bytes 8388608 | tf_op jit(solution)/shard_map/while/body/eval_jaxpr/psum | solution.py:176
  450.1 278.2 %copy-start.21 = (f32[2,512]{1,0:T(2,128)}, f32[2,512]{1,0:T(2,128)S(1)}, u32[]{:S(2)}) copy-start(f32[2,512]{1,0:T(2,128)S(1)} %add_rsqrt_fusion.5) | copy-start | bytes 12292 | tf_op jit(solution)/shard_map/while
  565.4 505.5 %reduce-scatter.19.cloned.1.call-start = ((), (), s32[]{:S(2)}) async-start(), calls=%async_computation.18 | async-start | bytes 18874368 | tf_op jit(solution)/shard_map/while/body/eval_jaxpr/reduce_scatter | solution.py:219
  955.7 429.0 %all-reduce.13.cloned.1.call-start = ((), (), s32[]{:S(2)}) async-start(), calls=%async_computation.19 | async-start | bytes 16777216 | tf_op jit(solution)/shard_map/while/body/eval_jaxpr/psum | solution.py:155
  1410.3 48.3 %all-gather.8.cloned.1.call-start = ((), (), s32[]{:S(2)}) async-start(), calls=%async_computation.12 | async-start | bytes 7077888 | tf_op jit(solution)/shard_map/while/body/eval_jaxpr/all_gather | solution.py:86
  1410.9 154.9 %all-gather.10.cloned.1.call-start = ((), (), s32[]{:S(2)}) async-start(), calls=%async_computation.13 | async-start | bytes 18874368 | tf_op jit(solution)/shard_map/while/body/eval_jaxpr/all_gather | solution.py:115
  1472.6 190.1 %all-gather.12.cloned.1.call-start = ((), (), s32[]{:S(2)}) async-start(), calls=%async_computation.14 | async-start | bytes 2359296 | tf_op jit(solution)/shard_map/while/body/eval_jaxpr/all_gather | solution.py:87
  1473.1 353.5 %all-reduce.9.cloned.1.call-start = ((), (), s32[]{:S(2)}) async-start(), calls=%async_computation.15 | async-start | bytes 8388608 | tf_op jit(solution)/shard_map/while/body/eval_jaxpr/psum | solution.py:140
  1669.0 212.9 %all-gather.6.cloned.1.call-start = ((), (), s32[]{:S(2)}) async-start(), calls=%async_computation.11 | async-start | bytes 9437184 | tf_op jit(solution)/shard_map/while/body/eval_jaxpr/all_gather | solution.py:88
  1669.5 251.5 %all-gather.14.cloned.1.call-start = ((), (), s32[]{:S(2)}) async-start(), calls=%async_computation.16 | async-start | bytes 4718592 | tf_op jit(solution)/shard_map/while/body/eval_jaxpr/all_gather | solution.py:89
  1670.1 431.8 %all-reduce.11.cloned.1.call-start = ((), (), s32[]{:S(2)}) async-start(), calls=%async_computation.17 | async-start | bytes 8388608 | tf_op jit(solution)/shard_map/while/body/eval_jaxpr/psum | solution.py:176
  1946.8 505.3 %reduce-scatter.19.cloned.1.call-start = ((), (), s32[]{:S(2)}) async-start(), calls=%async_computation.18 | async-start | bytes 18874368 | tf_op jit(solution)/shard_map/while/body/eval_jaxpr/reduce_scatter | solution.py:219
  2337.0 429.0 %all-reduce.13.cloned.1.call-start = ((), (), s32[]{:S(2)}) async-start(), calls=%async_computation.19 | async-start | bytes 16777216 | tf_op jit(solution)/shard_map/while/body/eval_jaxpr/psum | solution.py:155
  2793.8 37.3 %reduce-scatter.17.cloned.1.call-start = ((), (), s32[]{:S(2)}) async-start(), calls=%async_computation.10 | async-start | bytes 589824
  2795.7 80.6 %reduce-scatter.11.cloned.1.call-start = ((), (), s32[]{:S(2)}) async-start(), calls=%async_computation.7 | async-start | bytes 2359296 | tf_op jit(solution)/shard_map/reduce_scatter | solution.py:268
  2799.6 131.2 %reduce-scatter.15.cloned.1.call-start = ((), (), s32[]{:S(2)}) async-start(), calls=%async_computation.9 | async-start | bytes 4718592 | tf_op jit(solution)/shard_map/reduce_scatter | solution.py:274
  2805.7 190.4 %reduce-scatter.9.cloned.1.call-start = ((), (), s32[]{:S(2)}) async-start(), calls=%async_computation.6 | async-start | bytes 7077888 | tf_op jit(solution)/shard_map/reduce_scatter | solution.py:265
  2815.9 254.9 %reduce-scatter.13.cloned.1.call-start = ((), (), s32[]{:S(2)}) async-start(), calls=%async_computation.8 | async-start | bytes 9437184 | tf_op jit(solution)/shard_map/reduce_scatter | solution.py:271
  (87 other events, 3837.8 us)
Sparse Core Ops, SparseCore 0:
  27.8 49.3 all-gather.7
  91.2 93.1 all-gather.9
  186.4 28.1 all-gather.11
  287.6 157.5 all-reduce.8
  446.9 53.3 all-gather.5
  502.1 37.4 all-gather.13
  565.5 154.9 all-reduce.10
  955.8 114.9 reduce-scatter.18
  1093.2 291.5 all-reduce.12
  1412.9 45.6 all-gather.7
  1472.7 93.0 all-gather.9
  1567.7 28.1 all-gather.11
  1669.1 157.4 all-reduce.8
  1828.4 53.3 all-gather.5
  1883.5 37.4 all-gather.13
  1946.9 154.9 all-reduce.10
  2337.1 114.9 reduce-scatter.18
  2474.4 291.5 all-reduce.12
Sparse Core Ops, SparseCore 1:
  2798.0 33.1 reduce-scatter.16
  2835.2 41.1 reduce-scatter.10
  2879.6 51.2 reduce-scatter.14
  2934.6 61.5 reduce-scatter.8
  2999.6 71.1 reduce-scatter.12
where the time goes:
time: 3090 us; the launch traced here: 3080 us
  waiting for transfers between devices  1900 us (61%)
  matrix products  629 us (20%)
  other arithmetic  351 us (11%)
  local copies, waits for them, and re-layouts  158 us (5%)
    psum x2, waiting for transfers between devices, micro_step(): lax.psum(feedforward_part.astype(jnp.bfloat16), 'tensor')  487 us
    psum x2, waiting for transfers between devices, micro_step(): lax.psum(attention_part.astype(jnp.bfloat16), 'tensor').astype(jnp.float32)  313 us
    psum x2, waiting for transfers between devices, micro_step(): lax.psum(second_part.astype(jnp.bfloat16), 'tensor').astype(jnp.float32)  310 us
    all_gather x2, waiting for transfers between devices, micro_step(): all_pairs = lax.all_gather(key_value, 'context', axis=2, tiled=True)  174 us
    reduce_scatter x2, waiting for transfers between devices, micro_step(): lax.psum_scatter(spread.astype(jnp.bfloat16), 'context', scatter_dimensio...  165 us
    convert_element_type x2, other arithmetic, micro_step(): grad_scores = (probs * (grad_probs - row_dot)).astype(jnp.bfloat16)  133 us
    dot_general x2, matrix products, micro_step(): jnp.einsum('sqhe,skhe->shqk', grad_attended, value_buffer, preferred_elem...  108 us
    all_gather x2, waiting for transfers between devices, micro_step(): lax.all_gather(gateup_weight, 'context', axis=1, tiled=True)  101 us
  transfers between devices with their start and end apart: 23, of which 21 were waited for; matrix products, arithmetic and copies ran while one was open for 15% of the time, Pallas kernels for 0%

commit v1 on v0

--- a/solution.py
+++ b/solution.py
@@ -173,7 +173,9 @@
         second_part = jnp.einsum(
             "ksnf,kdf->snd", grad_gateup, gateup_full, preferred_element_type=jnp.float32
         )
-        grad_normed_two = lax.psum(second_part.astype(jnp.bfloat16), "tensor").astype(jnp.float32)
+        grad_normed_two = jnp.sum(
+            lax.all_gather(second_part.astype(jnp.bfloat16), "tensor"), axis=0
+        ).astype(jnp.float32)
         grad_rows_two, gain_two = norm_backward(
             grad_normed_two, normal_two, inverse_two, gains_value[1]
         )

time: 3090 us -> 3370 us (1.091)
  waiting for transfers between devices: 1900 us -> 2160 us
    all_gather x0 -> x2, waiting for transfers between devices: none -> 573 us  [micro_step(): lax.all_gather(second_part.astype(jnp.bfloat16), 'tensor')]
    psum x2 -> x0, waiting for transfers between devices: 310 us -> none  [micro_step(): lax.psum(second_part.astype(jnp.bfloat16), 'tensor').astype(jnp.float32)]
  transfers between devices with their start and end apart: 23 -> 23, of which waited for: 21 -> 21; matrix products, arithmetic and copies ran while one was open for 15% -> 13% of each run, Pallas kernels for 0% -> 0%
where the time goes in v1:
time: 3370 us
  waiting for transfers between devices  2160 us (64%)
  matrix products  629 us (19%)
  other arithmetic  374 us (11%)
  local copies, waits for them, and re-layouts  158 us (5%)
    all_gather x2, waiting for transfers between devices, micro_step(): lax.all_gather(second_part.astype(jnp.bfloat16), 'tensor')  573 us
    psum x2, waiting for transfers between devices, micro_step(): lax.psum(feedforward_part.astype(jnp.bfloat16), 'tensor')  487 us
    psum x2, waiting for transfers between devices, micro_step(): lax.psum(attention_part.astype(jnp.bfloat16), 'tensor').astype(jnp.float32)  313 us
    all_gather x2, waiting for transfers between devices, micro_step(): all_pairs = lax.all_gather(key_value, 'context', axis=2, tiled=True)  174 us
    reduce_scatter x2, waiting for transfers between devices, micro_step(): lax.psum_scatter(spread.astype(jnp.bfloat16), 'context', scatter_dimensio...  163 us
    convert_element_type x2, other arithmetic, micro_step(): grad_scores = (probs * (grad_probs - row_dot)).astype(jnp.bfloat16)  133 us
    dot_general x2, matrix products, micro_step(): jnp.einsum('sqhe,skhe->shqk', grad_attended, value_buffer, preferred_elem...  108 us
    all_gather x2, waiting for transfers between devices, micro_step(): lax.all_gather(gateup_weight, 'context', axis=1, tiled=True)  101 us
  transfers between devices with their start and end apart: 23, of which 21 were waited for; matrix products, arithmetic and copies ran while one was open for 13% of the time, Pallas kernels for 0%

profile of v1, /device:TPU:0, one launch (start us, length us, event | category | flops | bytes accessed | tf_op | source)
XLA Modules:
  0.0 3367.3 jit_solution(7327787402585358028)
XLA Ops:
  24.9 3054.8 %while.30 = (s32[]{:T(128)}, bf16[4,512,2048]{2,1,0:T(8,128)(2,1)}, f32[4,512,2048]{2,1,0:T(8,128)}, f32[3,2048,512]{1,2,0:T(8,128)}, f32[512,2048]{1,0:T(8,128)...) while((s32[]{:T(128)}, bf16[4,512,2048]{2,1,0:T(8,128)(2,1)}, ...), condition=%wide.region_17.18_spmd.clone.clone.clone, body=%wide.region_0.17_spmd.clone.clone.clone.sunk | while | flops 81186193408 | bytes 1969803776 | solution.py:262
  41.3 35.8 %all-gather.15.cloned.1.call-done = bf16[3,2048,512]{1,2,0:T(8,128)(2,1)} async-done(((bf16[3,256,512]{1,2,0:T(8,128)(2,1)}), bf16[3,2048,512]{1,2,0:T(8,128)(2,1)}) %all-gather.15.cloned.1.call-update) | async-done | bytes 6291472 | tf_op jit(solution)/shard_map/while/body/eval_jaxpr/all_gather | solution.py:86
  97.7 86.7 %all-gather.17.cloned.1.call-done = bf16[2,2,4096,512]{2,3,0,1:T(8,128)(2,1)} async-done(((bf16[2,2,512,512]{2,3,0,1:T(8,128)(2,1)}), bf16[2,2,4096,512]{2,3,0,1:T(8,128)(2,1)}) %all-gather.17.cloned.1.call-update) | async-done | bytes 16777232 | tf_op jit(solution)/shard_map/while/body/eval_jaxpr/all_gather | solution.py:115
  288.7 156.5 %all-reduce.8.cloned.1.call-done = bf16[2,512,2048]{2,1,0:T(8,128)(2,1)} async-done(((bf16[2,512,2048]{2,1,0:T(8,128)(2,1)}), bf16[2,512,2048]{2,1,0:T(8,128)(2,1)}) %all-reduce.8.cloned.1.call-update) | async-done | bytes 4194320 | tf_op jit(solution)/shard_map/while/body/eval_jaxpr/psum | solution.py:140
  450.1 50.3 %all-gather.13.cloned.1.call-done = bf16[2,2048,1024]{2,1,0:T(8,128)(2,1)} async-done(((bf16[2,256,1024]{2,1,0:T(8,128)(2,1)}), bf16[2,2048,1024]{2,1,0:T(8,128)(2,1)}) %all-gather.13.cloned.1.call-update) | async-done | bytes 8388624 | tf_op jit(solution)/shard_map/while/body/eval_jaxpr/all_gather | solution.py:88
  565.6 286.7 %all-gather.23.cloned.1.call-done = bf16[8,512,2048]{2,1,0:T(8,128)(2,1)} async-done(((bf16[2,512,2048]{2,1,0:T(8,128)(2,1)}), bf16[8,512,2048]{2,1,0:T(8,128)(2,1)}) %all-gather.23.cloned.1.call-update) | async-done | bytes 16777232 | tf_op jit(solution)/shard_map/while/body/eval_jaxpr/all_gather | solution.py:177
  881.8 53.9 %multiply_reduce_fusion.5 = (f32[2,8,512]{2,1,0:T(8,128)S(1)}, f32[2,8,512,2560]{3,2,1,0:T(8,128)}) fusion(f32[2,8,512,2560]{3,2,1,0:T(8,128)} %get-tuple-element.1033, f32[2,8,512]{2,1,0:T(8,128)S(1)} %log_add_fusion.2, bf16[2,512,8,64]{1,3,2,0:T(8,128)(2,1)S(1)} %bitcast.273, bf16[2,2560,8,64]{1,3,2,0:T(8,128)(2,1)S(1)} %bitcast.268), kind=kOutput, calls=%fused_computation.5.clone.1 | convolution fusion | flops 2747260928 | bytes 174129152 | tf_op jit(solution)/shard_map/while/body/eval_jaxpr/sqhe,skhe->shqk/dot_general | solution.py:200
  967.1 66.3 %multiply_convert_fusion.8 = bf16[2,8,512,2560]{3,2,1,0:T(8,128)(2,1)} fusion(f32[2,8,512,2560]{3,2,1,0:T(8,128)} %get-tuple-element.1040, f32[2,8,512,2560]{3,2,1,0:T(8,128)} %get-tuple-element.1033, f32[2,8,512]{2,1,0:T(8,128)S(1)} %get-tuple-element.1041, f32[2,8,512]{2,1,0:T(8,128)S(1)} %log_add_fusion.2), kind=kLoop, calls=%fused_computation.4.clone.1 | loop fusion | flops 83886080 | bytes 209780736 | tf_op jit(solution)/shard_map/while/body/eval_jaxpr/convert_element_type | solution.py:204
  1131.9 81.7 %reduce-scatter.19.cloned.1.call-done = bf16[2,2,512,512]{3,2,0,1:T(8,128)(2,1)} async-done(((bf16[2,2,4096,512]{3,2,0,1:T(8,128)(2,1)}), bf16[2,2,512,512]{3,2,0,1:T(8,128)(2,1)}) %reduce-scatter.19.cloned.1.call-update) | async-done | bytes 2097168 | tf_op jit(solution)/shard_map/while/body/eval_jaxpr/reduce_scatter | solution.py:221
  1280.0 247.5 %all-reduce.10.cloned.1.call-done = (bf16[2,512,2048]{2,1,0:T(8,128)(2,1)}, bf16[2,512,2048]{2,1,0:T(8,128)(2,1)}) async-done(((bf16[2,512,2048]{2,1,0:T(8,128)(2,1)}, bf16[2,512,2048]{2,1,0:T(8,128)(2,1)}), (bf16[2,512,2048]{2,1,0:T(8,128)(2,1)}, bf16[2,512,2048]{2,1,0:T(8,128)(2,1)})) %all-reduce.10.cloned.1.call-update) | async-done | bytes 8388624 | tf_op jit(solution)/shard_map/while/body/eval_jaxpr/psum | solution.py:155
  1567.8 33.7 %all-gather.15.cloned.1.call-done = bf16[3,2048,512]{1,2,0:T(8,128)(2,1)} async-done(((bf16[3,256,512]{1,2,0:T(8,128)(2,1)}), bf16[3,2048,512]{1,2,0:T(8,128)(2,1)}) %all-gather.15.cloned.1.call-update) | async-done | bytes 6291472 | tf_op jit(solution)/shard_map/while/body/eval_jaxpr/all_gather | solution.py:86
  1621.5 87.2 %all-gather.17.cloned.1.call-done = bf16[2,2,4096,512]{2,3,0,1:T(8,128)(2,1)} async-done(((bf16[2,2,512,512]{2,3,0,1:T(8,128)(2,1)}), bf16[2,2,4096,512]{2,3,0,1:T(8,128)(2,1)}) %all-gather.17.cloned.1.call-update) | async-done | bytes 16777232 | tf_op jit(solution)/shard_map/while/body/eval_jaxpr/all_gather | solution.py:115
  1715.9 32.9 fusion.193
  1813.1 156.4 %all-reduce.8.cloned.1.call-done = bf16[2,512,2048]{2,1,0:T(8,128)(2,1)} async-done(((bf16[2,512,2048]{2,1,0:T(8,128)(2,1)}), bf16[2,512,2048]{2,1,0:T(8,128)(2,1)}) %all-reduce.8.cloned.1.call-update) | async-done | bytes 4194320 | tf_op jit(solution)/shard_map/while/body/eval_jaxpr/psum | solution.py:140
  1974.4 50.3 %all-gather.13.cloned.1.call-done = bf16[2,2048,1024]{2,1,0:T(8,128)(2,1)} async-done(((bf16[2,256,1024]{2,1,0:T(8,128)(2,1)}), bf16[2,2048,1024]{2,1,0:T(8,128)(2,1)}) %all-gather.13.cloned.1.call-update) | async-done | bytes 8388624 | tf_op jit(solution)/shard_map/while/body/eval_jaxpr/all_gather | solution.py:88
  2090.1 286.5 %all-gather.23.cloned.1.call-done = bf16[8,512,2048]{2,1,0:T(8,128)(2,1)} async-done(((bf16[2,512,2048]{2,1,0:T(8,128)(2,1)}), bf16[8,512,2048]{2,1,0:T(8,128)(2,1)}) %all-gather.23.cloned.1.call-update) | async-done | bytes 16777232 | tf_op jit(solution)/shard_map/while/body/eval_jaxpr/all_gather | solution.py:177
  2406.1 53.9 %multiply_reduce_fusion.5 = (f32[2,8,512]{2,1,0:T(8,128)S(1)}, f32[2,8,512,2560]{3,2,1,0:T(8,128)}) fusion(f32[2,8,512,2560]{3,2,1,0:T(8,128)} %get-tuple-element.1033, f32[2,8,512]{2,1,0:T(8,128)S(1)} %log_add_fusion.2, bf16[2,512,8,64]{1,3,2,0:T(8,128)(2,1)S(1)} %bitcast.273, bf16[2,2560,8,64]{1,3,2,0:T(8,128)(2,1)S(1)} %bitcast.268), kind=kOutput, calls=%fused_computation.5.clone.1 | convolution fusion | flops 2747260928 | bytes 174129152 | tf_op jit(solution)/shard_map/while/body/eval_jaxpr/sqhe,skhe->shqk/dot_general | solution.py:200
  2491.2 66.3 %multiply_convert_fusion.8 = bf16[2,8,512,2560]{3,2,1,0:T(8,128)(2,1)} fusion(f32[2,8,512,2560]{3,2,1,0:T(8,128)} %get-tuple-element.1040, f32[2,8,512,2560]{3,2,1,0:T(8,128)} %get-tuple-element.1033, f32[2,8,512]{2,1,0:T(8,128)S(1)} %get-tuple-element.1041, f32[2,8,512]{2,1,0:T(8,128)S(1)} %log_add_fusion.2), kind=kLoop, calls=%fused_computation.4.clone.1 | loop fusion | flops 83886080 | bytes 209780736 | tf_op jit(solution)/shard_map/while/body/eval_jaxpr/convert_element_type | solution.py:204
  2656.1 81.7 %reduce-scatter.19.cloned.1.call-done = bf16[2,2,512,512]{3,2,0,1:T(8,128)(2,1)} async-done(((bf16[2,2,4096,512]{3,2,0,1:T(8,128)(2,1)}), bf16[2,2,512,512]{3,2,0,1:T(8,128)(2,1)}) %reduce-scatter.19.cloned.1.call-update) | async-done | bytes 2097168 | tf_op jit(solution)/shard_map/while/body/eval_jaxpr/reduce_scatter | solution.py:221
  2812.0 239.6 %all-reduce.10.cloned.1.call-done = (bf16[2,512,2048]{2,1,0:T(8,128)(2,1)}, bf16[2,512,2048]{2,1,0:T(8,128)(2,1)}) async-done(((bf16[2,512,2048]{2,1,0:T(8,128)(2,1)}, bf16[2,512,2048]{2,1,0:T(8,128)(2,1)}), (bf16[2,512,2048]{2,1,0:T(8,128)(2,1)}, bf16[2,512,2048]{2,1,0:T(8,128)(2,1)})) %all-reduce.10.cloned.1.call-update) | async-done | bytes 8388624 | tf_op jit(solution)/shard_map/while/body/eval_jaxpr/psum | solution.py:155
  3118.5 43.7 %reduce-scatter.11.cloned.1.call-done = bf16[512,256]{1,0:T(8,128)(2,1)} async-done(((bf16[512,2048]{1,0:T(8,128)(2,1)}), bf16[512,256]{1,0:T(8,128)(2,1)}) %reduce-scatter.11.cloned.1.call-update) | async-done | bytes 262160 | tf_op jit(solution)/shard_map/reduce_scatter | solution.py:270
  3164.0 52.7 %reduce-scatter.15.cloned.1.call-done = bf16[1024,256]{1,0:T(8,128)(2,1)} async-done(((bf16[1024,2048]{1,0:T(8,128)(2,1)}), bf16[1024,256]{1,0:T(8,128)(2,1)}) %reduce-scatter.15.cloned.1.call-update) | async-done | bytes 524304 | tf_op jit(solution)/shard_map/reduce_scatter | solution.py:276
  3218.7 63.3 %reduce-scatter.9.cloned.1.call-done = bf16[3,256,512]{2,1,0:T(8,128)(2,1)} async-done(((bf16[3,2048,512]{2,1,0:T(8,128)(2,1)}), bf16[3,256,512]{2,1,0:T(8,128)(2,1)}) %reduce-scatter.9.cloned.1.call-update) | async-done | bytes 786448 | tf_op jit(solution)/shard_map/reduce_scatter | solution.py:267
  3284.5 72.2 %reduce-scatter.13.cloned.1.call-done = bf16[2,256,1024]{2,1,0:T(8,128)(2,1)} async-done(((bf16[2,2048,1024]{2,1,0:T(8,128)(2,1)}), bf16[2,256,1024]{2,1,0:T(8,128)(2,1)}) %reduce-scatter.13.cloned.1.call-update) | async-done | bytes 1048592 | tf_op jit(solution)/shard_map/reduce_scatter | solution.py:273
  (375 shorter events, 961.4 us)
Async XLA Ops:
  24.9 52.3 %all-gather.15.cloned.1.call-start = ((), (), s32[]{:S(2)}) async-start(), calls=%async_computation.12 | async-start | bytes 7077888 | tf_op jit(solution)/shard_map/while/body/eval_jaxpr/all_gather | solution.py:86
  25.6 158.7 %all-gather.17.cloned.1.call-start = ((), (), s32[]{:S(2)}) async-start(), calls=%async_computation.13 | async-start | bytes 18874368 | tf_op jit(solution)/shard_map/while/body/eval_jaxpr/all_gather | solution.py:115
  91.1 190.1 %all-gather.19.cloned.1.call-start = ((), (), s32[]{:S(2)}) async-start(), calls=%async_computation.14 | async-start | bytes 2359296 | tf_op jit(solution)/shard_map/while/body/eval_jaxpr/all_gather | solution.py:87
  91.8 353.3 %all-reduce.8.cloned.1.call-start = ((), (), s32[]{:S(2)}) async-start(), calls=%async_computation.15 | async-start | bytes 8388608 | tf_op jit(solution)/shard_map/while/body/eval_jaxpr/psum | solution.py:140
  287.5 212.9 %all-gather.13.cloned.1.call-start = ((), (), s32[]{:S(2)}) async-start(), calls=%async_computation.11 | async-start | bytes 9437184 | tf_op jit(solution)/shard_map/while/body/eval_jaxpr/all_gather | solution.py:88
  288.1 251.5 %all-gather.21.cloned.1.call-start = ((), (), s32[]{:S(2)}) async-start(), calls=%async_computation.16 | async-start | bytes 4718592 | tf_op jit(solution)/shard_map/while/body/eval_jaxpr/all_gather | solution.py:89
  288.7 563.6 %all-gather.23.cloned.1.call-start = ((), (), s32[]{:S(2)}) async-start(), calls=%async_computation.17 | async-start | bytes 20971520 | tf_op jit(solution)/shard_map/while/body/eval_jaxpr/all_gather | solution.py:177
  450.1 421.5 %copy-start.21 = (f32[2,512]{1,0:T(2,128)}, f32[2,512]{1,0:T(2,128)S(1)}, u32[]{:S(2)}) copy-start(f32[2,512]{1,0:T(2,128)S(1)} %add_rsqrt_fusion.5) | copy-start | bytes 12292 | tf_op jit(solution)/shard_map/while
  565.3 648.3 %reduce-scatter.19.cloned.1.call-start = ((), (), s32[]{:S(2)}) async-start(), calls=%async_computation.18 | async-start | bytes 18874368 | tf_op jit(solution)/shard_map/while/body/eval_jaxpr/reduce_scatter | solution.py:221
  1099.3 428.2 %all-reduce.10.cloned.1.call-start = ((), (), s32[]{:S(2)}) async-start(), calls=%async_computation.19 | async-start | bytes 16777216 | tf_op jit(solution)/shard_map/while/body/eval_jaxpr/psum | solution.py:155
  1553.2 48.3 %all-gather.15.cloned.1.call-start = ((), (), s32[]{:S(2)}) async-start(), calls=%async_computation.12 | async-start | bytes 7077888 | tf_op jit(solution)/shard_map/while/body/eval_jaxpr/all_gather | solution.py:86
  1553.8 154.9 %all-gather.17.cloned.1.call-start = ((), (), s32[]{:S(2)}) async-start(), calls=%async_computation.13 | async-start | bytes 18874368 | tf_op jit(solution)/shard_map/while/body/eval_jaxpr/all_gather | solution.py:115
  1615.4 190.1 %all-gather.19.cloned.1.call-start = ((), (), s32[]{:S(2)}) async-start(), calls=%async_computation.14 | async-start | bytes 2359296 | tf_op jit(solution)/shard_map/while/body/eval_jaxpr/all_gather | solution.py:87
  1616.0 353.5 %all-reduce.8.cloned.1.call-start = ((), (), s32[]{:S(2)}) async-start(), calls=%async_computation.15 | async-start | bytes 8388608 | tf_op jit(solution)/shard_map/while/body/eval_jaxpr/psum | solution.py:140
  1811.8 212.9 %all-gather.13.cloned.1.call-start = ((), (), s32[]{:S(2)}) async-start(), calls=%async_computation.11 | async-start | bytes 9437184 | tf_op jit(solution)/shard_map/while/body/eval_jaxpr/all_gather | solution.py:88
  1812.4 251.5 %all-gather.21.cloned.1.call-start = ((), (), s32[]{:S(2)}) async-start(), calls=%async_computation.16 | async-start | bytes 4718592 | tf_op jit(solution)/shard_map/while/body/eval_jaxpr/all_gather | solution.py:89
  1813.0 563.6 %all-gather.23.cloned.1.call-start = ((), (), s32[]{:S(2)}) async-start(), calls=%async_computation.17 | async-start | bytes 20971520 | tf_op jit(solution)/shard_map/while/body/eval_jaxpr/all_gather | solution.py:177
  2089.7 648.1 %reduce-scatter.19.cloned.1.call-start = ((), (), s32[]{:S(2)}) async-start(), calls=%async_computation.18 | async-start | bytes 18874368 | tf_op jit(solution)/shard_map/while/body/eval_jaxpr/reduce_scatter | solution.py:221
  2623.4 428.2 %all-reduce.10.cloned.1.call-start = ((), (), s32[]{:S(2)}) async-start(), calls=%async_computation.19 | async-start | bytes 16777216 | tf_op jit(solution)/shard_map/while/body/eval_jaxpr/psum | solution.py:155
  3079.7 37.3 %reduce-scatter.17.cloned.1.call-start = ((), (), s32[]{:S(2)}) async-start(), calls=%async_computation.10 | async-start | bytes 589824
  3081.6 80.6 %reduce-scatter.11.cloned.1.call-start = ((), (), s32[]{:S(2)}) async-start(), calls=%async_computation.7 | async-start | bytes 2359296 | tf_op jit(solution)/shard_map/reduce_scatter | solution.py:270
  3085.5 131.2 %reduce-scatter.15.cloned.1.call-start = ((), (), s32[]{:S(2)}) async-start(), calls=%async_computation.9 | async-start | bytes 4718592 | tf_op jit(solution)/shard_map/reduce_scatter | solution.py:276
  3091.6 190.4 %reduce-scatter.9.cloned.1.call-start = ((), (), s32[]{:S(2)}) async-start(), calls=%async_computation.6 | async-start | bytes 7077888 | tf_op jit(solution)/shard_map/reduce_scatter | solution.py:267
  3101.7 254.9 %reduce-scatter.13.cloned.1.call-start = ((), (), s32[]{:S(2)}) async-start(), calls=%async_computation.8 | async-start | bytes 9437184 | tf_op jit(solution)/shard_map/reduce_scatter | solution.py:273
  (87 other events, 3978.5 us)
Sparse Core Ops, SparseCore 0:
  27.8 49.3 all-gather.14
  91.2 93.1 all-gather.16
  186.4 28.1 all-gather.18
  287.6 157.5 all-reduce.7
  446.9 53.3 all-gather.12
  502.1 37.4 all-gather.20
  565.4 286.7 all-gather.22
  1099.4 114.1 reduce-scatter.18
  1235.9 291.5 all-reduce.9
  1555.8 45.6 all-gather.14
  1615.6 93.1 all-gather.16
  1710.6 28.1 all-gather.18
  1812.0 157.5 all-reduce.7
  1971.3 53.3 all-gather.12
  2026.4 37.4 all-gather.20
  2089.8 286.7 all-gather.22
  2623.5 114.1 reduce-scatter.18
  2760.0 291.5 all-reduce.9
Sparse Core Ops, SparseCore 1:
  3083.8 33.1 reduce-scatter.16
  3121.1 41.1 reduce-scatter.10
  3165.4 51.2 reduce-scatter.14
  3220.4 61.5 reduce-scatter.8
  3285.5 71.1 reduce-scatter.12
